TPU v7x, 256 devices: a whole 4x4x8 slice. The times are simulated.
256 devices in a mesh: dp: 4 (over y), expert: 64 (over x, z, core).
Axes of the slice: x: 4, y: 4, z: 8, core: 2. Of those that a mesh axis runs over, the one named last changes fastest.
Arguments:
- unit_codes: bfloat16 [128, 256, 1536], P('expert', 'dp'), may hold values from -4 to 4
- block_scales: float32 [128, 12, 256], P('expert', None, 'dp'), may hold values from 0.05 to 2
- pair_list: int32 [2048, 2], replicated, may hold values from 0 to 127, as said below
Outputs:
- left_best: float32 [64, 32, 1536], P('expert', None, 'dp')
- right_best: float32 [64, 32, 1536], P('expert', None, 'dp')
Inputs may be any that keep to these rules, and one draw needn't show every extreme that they name: `pair_list`: row 32 * e + s names as its first expert one of 2 * e to 2 * e + 1, and as its second one of the 2 experts starting at 2 * ((e + o_s) mod n), with n = 64; the offsets o_s are nonzero, distinct over s, include 1, n / 2 and n - 1, and are the same for every e.
All inputs are finite; a program needn't handle non-finite values.
Results may differ from a plain program's by a relative error of at most 0.0017.
Values may be sent and summed in bfloat16 or wider, within the bound.
No kernel may reach another device: no remote copies, remote signals or barrier semaphores. Data moves between devices by JAX's collectives and lax.ppermute only.
A program may use at most 128 MiB of HBM per device.

v0:
```python
import math
import jax
import jax.numpy as jnp
from jax import lax
from jax.sharding import PartitionSpec as P

EPSILON = 1e-06


def body(unit_codes, block_scales, pair_list):
    num_devices = lax.axis_size("expert")
    groups = lax.axis_size("dp")
    my_index = lax.axis_index("expert")
    dp_index = lax.axis_index("dp")
    per_device, row_count, unit_count = unit_codes.shape
    num_blocks = block_scales.shape[1]
    block_len = unit_count // num_blocks
    slice_width = unit_count // groups
    factor = jnp.transpose(block_scales, (0, 2, 1))[:, :, :, None]
    acts = (
        unit_codes.astype(jnp.float32).reshape(per_device, row_count, num_blocks, block_len)
        * factor
    )
    acts = acts.reshape(per_device, row_count, unit_count).astype(jnp.bfloat16)
    slot_count = pair_list.shape[0] // num_devices
    pair_table = pair_list.reshape(num_devices, slot_count, 2)
    my_pairs = lax.dynamic_index_in_dim(pair_table, my_index, 0, keepdims=False)
    left_local = my_pairs[:, 0] % per_device
    right_dev = my_pairs[:, 1] // per_device
    is_asked = pair_table[:, :, 1] // per_device == my_index
    chosen = jnp.sum(jnp.where(is_asked, pair_table[:, :, 1] % per_device, 0), axis=1)
    in_use = jnp.any(is_asked, axis=1)
    chooser = ((chosen[:, None] == jnp.arange(per_device)[None, :]) & in_use[:, None]).astype(
        jnp.bfloat16
    )
    own_full = lax.all_gather(acts, "dp", axis=1, tiled=True)
    flattened = acts.reshape(per_device, -1)
    outbound = jnp.dot(chooser, flattened, preferred_element_type=jnp.float32).astype(jnp.bfloat16)
    received = lax.all_to_all(
        outbound.reshape((num_devices,) + acts.shape[1:]),
        "expert",
        split_axis=0,
        concat_axis=0,
        tiled=True,
    )
    wanted = jnp.take(received, right_dev, axis=0)
    partner = lax.all_to_all(wanted, "dp", split_axis=2, concat_axis=1, tiled=True)
    all_rows = partner.shape[1]
    own_square = (
        jnp.einsum("era,era->ea", own_full, own_full, preferred_element_type=jnp.float32) / all_rows
    )
    inv_own = 1.0 / jnp.sqrt(own_square + EPSILON)
    part_square = (
        jnp.einsum("srb,srb->sb", partner, partner, preferred_element_type=jnp.float32) / all_rows
    )
    inv_part = 1.0 / jnp.sqrt(part_square + EPSILON)

    def single(member):
        expert_pick, partner_block, inv_unit = member
        left_rows = jnp.take(own_full, expert_pick, axis=0)
        gram_block = jnp.einsum(
            "ra,rb->ab", left_rows, partner_block, preferred_element_type=jnp.float32
        )
        correlation = (
            gram_block
            / all_rows
            * jnp.take(inv_own, expert_pick, axis=0)[:, None]
            * inv_unit[None, :]
        )
        return (jnp.max(correlation, axis=1), jnp.max(correlation, axis=0))

    def several(member):
        return jax.vmap(single)(member)

    bundle = math.gcd(slot_count, 4)
    stacked = (
        left_local.reshape(-1, bundle),
        partner.reshape(-1, bundle, all_rows, slice_width),
        inv_part.reshape(-1, bundle, slice_width),
    )
    left_part, right_part = lax.map(several, stacked)
    left_part = left_part.reshape(slot_count, unit_count)
    right_part = right_part.reshape(slot_count, slice_width)
    left_all = lax.pmax(left_part, "dp")
    left_out = lax.dynamic_slice_in_dim(left_all, dp_index * slice_width, slice_width, 1)
    target = (right_dev[:, None] == jnp.arange(num_devices)[None, :]).astype(jnp.float32)
    outgoing = jnp.dot(
        target.T, right_part, precision=lax.Precision.HIGHEST, preferred_element_type=jnp.float32
    )
    returned = lax.all_to_all(outgoing, "expert", split_axis=0, concat_axis=0, tiled=True)
    offsets = pair_table[0, :, 1] // per_device
    source_dev = (my_index - offsets) % num_devices
    right_out = jnp.take(returned, source_dev, axis=0)
    return (left_out[None], right_out[None])


def solution(mesh):
    in_specs = (P("expert", "dp", None), P("expert", None, "dp"), P())
    out_specs = (P("expert", None, "dp"), P("expert", None, "dp"))
    return jax.shard_map(body, mesh=mesh, in_specs=in_specs, out_specs=out_specs, check_vma=False)
```

profile of v0, /device:TPU:2, one launch (start us, length us, event | category | flops | bytes accessed | tf_op | source)
XLA Modules:
  0.0 609.7 jit_solution(17279301070880780680)
XLA Ops:
  14.7 7.1 %copy.53 = bf16[8,8,64,1536]{3,2,1,0:T(8,128)(2,1)} copy(bf16[8,8,64,1536]{3,1,2,0:T(8,128)(2,1)S(1)} %bitcast.117) | data formatting | bytes 25165824
  21.8 12.2 %all-to-all-start = ((bf16[64,64,1536]{2,1,0:T(8,128)(2,1)}), bf16[64,64,1536]{2,1,0:T(8,128)(2,1)}, u32[]{:S(2)}, u32[]{:S(2)}) async-start(bf16[64,64,1536]{2,1,0:T(8,128)(2,1)} %bitcast.116), calls=%async_computation | async-start | bytes 25165824 | tf_op jit(solution)/shard_map/all_to_all | solution.py:39
  34.1 274.5 %all-to-all-done = bf16[64,64,1536]{2,1,0:T(8,128)(2,1)} async-done(((bf16[64,64,1536]{2,1,0:T(8,128)(2,1)}), bf16[64,64,1536]{2,1,0:T(8,128)(2,1)}, u32[]{:S(2)}, u32[]{:S(2)}) %all-to-all-start) | async-done | bytes 12582944 | tf_op jit(solution)/shard_map/all_to_all | solution.py:39
  308.6 8.1 %gather_fusion.2 = bf16[32,64,1536]{2,1,0:T(8,128)(2,1)} fusion(bf16[64,64,1536]{2,1,0:T(8,128)(2,1)} %all-to-all-done, s32[1024]{0:T(1024)S(1)} %pad_clamp_fusion.2), kind=kCustom, calls=%fused_computation.2 | custom fusion | bytes 12583040 | tf_op jit(solution)/shard_map/jit(_take)/gather | solution.py:46
  316.7 6.1 broadcast_select_fusion
  322.8 18.4 %copy.29 = bf16[32,64,1536]{1,0,2:T(8,128)(2,1)} copy(bf16[32,64,1536]{2,1,0:T(8,128)(2,1)} %broadcast_select_fusion) | data formatting | bytes 12582912 | tf_op jit(solution)/shard_map/jit(_take)/select_n | solution.py:46
  341.2 12.8 %reshape.286 = bf16[4,2,393216]{2,1,0:T(2,128)(2,1)} reshape(bf16[1536,32,64]{2,1,0:T(8,128)(2,1)} %bitcast.118) | data formatting | bytes 12582912
  354.0 5.3 all-to-all-start.1
  360.2 41.9 %all-gather.2.cloned.1.call-done = bf16[2,256,1536]{2,1,0:T(8,128)(2,1)} async-done(((bf16[2,64,1536]{2,1,0:T(8,128)(2,1)}), bf16[2,256,1536]{2,1,0:T(8,128)(2,1)}) %all-gather.2.cloned.1.call-update) | async-done | bytes 1572880 | tf_op jit(solution)/shard_map/all_gather | solution.py:36
  403.9 40.7 %all-to-all-done.1 = bf16[4,2,393216]{2,1,0:T(2,128)(2,1)} async-done(((bf16[4,2,393216]{2,1,0:T(2,128)(2,1)}), bf16[4,2,393216]{2,1,0:T(2,128)(2,1)}, u32[]{:S(2)}, u32[]{:S(2)}) %all-to-all-start.1) | async-done | bytes 6291488 | tf_op jit(solution)/shard_map/all_to_all | solution.py:47
  444.5 12.6 %reshape.287 = bf16[1536,32,64]{2,1,0:T(8,128)(2,1)} reshape(bf16[4,2,393216]{2,1,0:T(2,128)(2,1)} %all-to-all-done.1) | data formatting | bytes 12582912
  457.2 15.1 %copy.45 = bf16[32,64,4,384]{3,2,1,0:T(4,128)(2,1)} copy(bf16[32,64,4,384]{1,0,3,2:T(8,128)(2,1)} %bitcast.119) | data formatting | bytes 12582912 | tf_op jit(solution)/shard_map/all_to_all | solution.py:47
  481.3 64.2 %while.12 = (s32[]{:T(128)}, f32[8,4,1536]{2,1,0:T(4,128)S(1)}, f32[8,4,384]{2,1,0:T(4,128)S(1)}, s32[8,4]{1,0:T(8,128)S(1)}, bf16[2,256,1536]{2,1,0:T(8,128)(2,...) while((s32[]{:T(128)}, f32[8,4,1536]{2,1,0:T(4,128)S(1)}, ...), condition=%wide.region_5.6_spmd, body=%wide.region_2.5_spmd.sunk | while | flops 1218975232 | bytes 10461917 | solution.py:81
  484.4 4.8 fusion.37
  492.4 4.8 fusion.37
  500.5 4.8 fusion.37
  508.5 4.8 fusion.37
  516.5 4.8 fusion.37
  524.5 4.8 fusion.37
  532.6 4.8 fusion.37
  540.6 4.8 fusion.37
  546.5 5.8 all-to-all-start.2
  553.2 8.4 %all-to-all-done.2 = f32[64,1,384]{2,1,0:T(1,128)S(1)} async-done(((f32[64,1,384]{2,1,0:T(1,128)}), f32[64,1,384]{2,1,0:T(1,128)S(1)}, u32[]{:S(2)}, u32[]{:S(2)}) %all-to-all-start.2) | async-done | bytes 98336 | tf_op jit(solution)/shard_map/all_to_all | solution.py:90
  562.8 38.6 %all-reduce.2.cloned.1.call-done = f32[32,1536]{1,0:T(8,128)} async-done(((f32[32,1536]{1,0:T(8,128)}), f32[32,1536]{1,0:T(8,128)}) %all-reduce.2.cloned.1.call-update) | async-done | bytes 196624 | tf_op jit(solution)/shard_map/pmax | solution.py:84
  (117 shorter events, 48.9 us)
Async XLA Ops:
  10.3 4.4 copy-start.2
  21.8 286.8 %all-to-all-start = ((bf16[64,64,1536]{2,1,0:T(8,128)(2,1)}), bf16[64,64,1536]{2,1,0:T(8,128)(2,1)}, u32[]{:S(2)}, u32[]{:S(2)}) async-start(bf16[64,64,1536]{2,1,0:T(8,128)(2,1)} %bitcast.116), calls=%async_computation | async-start | bytes 25165824 | tf_op jit(solution)/shard_map/all_to_all | solution.py:39
  354.0 90.5 %all-to-all-start.1 = ((bf16[4,2,393216]{2,1,0:T(2,128)(2,1)}), bf16[4,2,393216]{2,1,0:T(2,128)(2,1)}, u32[]{:S(2)}, u32[]{:S(2)}) async-start(bf16[4,2,393216]{2,1,0:T(2,128)(2,1)} %reshape.286), calls=%async_computation.1 | async-start | bytes 12582912 | tf_op jit(solution)/shard_map/all_to_all | solution.py:47
  359.3 42.8 %all-gather.2.cloned.1.call-start = ((), (), s32[]{:S(2)}) async-start(), calls=%async_computation.3 | async-start | bytes 1966080 | tf_op jit(solution)/shard_map/all_gather | solution.py:36
  476.6 2.7 copy-start.1
  479.3 2.0 copy-start
  546.5 15.0 %all-to-all-start.2 = ((f32[64,1,384]{2,1,0:T(1,128)}), f32[64,1,384]{2,1,0:T(1,128)S(1)}, u32[]{:S(2)}, u32[]{:S(2)}) async-start(f32[64,1,384]{2,1,0:T(1,128)} %copy.33), calls=%async_computation.2 | async-start | bytes 196608 | tf_op jit(solution)/shard_map/all_to_all | solution.py:90
  552.3 49.1 %all-reduce.2.cloned.1.call-start = ((), (), s32[]{:S(2)}) async-start(), calls=%async_computation.4 | async-start | bytes 393216 | tf_op jit(solution)/shard_map/pmax | solution.py:84
Sparse Core Ops, SparseCore 0:
  361.9 40.1 all-gather.1
  555.5 45.8 all-reduce.1
where the time goes:
time: 611 us; the launch traced here: 610 us
  waiting for transfers between devices  405 us (66%)
  local copies, waits for them, and re-layouts  112 us (18%)
  matrix products  42.6 us (7%)
  starting transfers between devices  23.5 us (4%)
  between operations  14.3 us (2%)
  other arithmetic  12.7 us (2%)
    all_to_all x1, waiting for transfers between devices, body(): lax.all_to_all(outbound.reshape((num_devices,) + acts.shape[1:]), 'expert...  274 us
    all_gather x1, waiting for transfers between devices, body(): own_full = lax.all_gather(acts, 'dp', axis=1, tiled=True)  41.9 us
    all_to_all x1, waiting for transfers between devices, body(): lax.all_to_all(wanted, 'dp', split_axis=2, concat_axis=1, tiled=True)  40.7 us
    dot_general x8, matrix products, single(): jnp.einsum('ra,rb->ab', left_rows, partner_block, preferred_element_type=...  38.6 us
    pmax x1, waiting for transfers between devices, body(): left_all = lax.pmax(left_part, 'dp')  38.6 us
    unnamed x11, local copies, waits for them, and re-layouts  35.6 us
    gather x8, local copies, waits for them, and re-layouts, single(): left_rows = jnp.take(own_full, expert_pick, axis=0)  19.6 us
    all_to_all x2, local copies, waits for them, and re-layouts, body(): lax.all_to_all(wanted, 'dp', split_axis=2, concat_axis=1, tiled=True)  19.4 us
  transfers between devices with their start and end apart: 5, of which 5 were waited for; matrix products, arithmetic and copies ran while one was open for 1% of the time, Pallas kernels for 0%

commit v1 on v0

--- a/solution.py
+++ b/solution.py
@@ -44,7 +44,10 @@
         tiled=True,
     )
     wanted = jnp.take(received, right_dev, axis=0)
-    partner = lax.all_to_all(wanted, "dp", split_axis=2, concat_axis=1, tiled=True)
+    partner = jnp.concatenate(
+        lax.all_to_all(jnp.stack(jnp.split(wanted, lax.axis_size("dp"), axis=2)), "dp", 0, 0),
+        axis=1,
+    )
     all_rows = partner.shape[1]
     own_square = (
         jnp.einsum("era,era->ea", own_full, own_full, preferred_element_type=jnp.float32) / all_rows

time: 611 us -> 553 us (0.905)
  local copies, waits for them, and re-layouts: 112 us -> 53.2 us
    unnamed x11 -> x9, local copies, waits for them, and re-layouts: 35.6 us -> 10.2 us
    select_n x1 -> x0, local copies, waits for them, and re-layouts: 18.4 us -> none  [body(): wanted = jnp.take(received, right_dev, axis=0)]
    all_to_all x2 -> x1, local copies, waits for them, and re-layouts: 19.4 us -> 3.59 us  [body(): lax.all_to_all(jnp.stack(jnp.split(wanted, lax.axis_size('dp'), axis=2)),...]
where the time goes in v1:
time: 553 us; the launch traced here: 552 us
  waiting for transfers between devices  405 us (73%)
  local copies, waits for them, and re-layouts  53.2 us (10%)
  matrix products  42.6 us (8%)
  starting transfers between devices  23.5 us (4%)
  between operations  14.3 us (3%)
  other arithmetic  13.6 us (2%)
    all_to_all x1, waiting for transfers between devices, body(): lax.all_to_all(outbound.reshape((num_devices,) + acts.shape[1:]), 'expert...  274 us
    all_gather x1, waiting for transfers between devices, body(): own_full = lax.all_gather(acts, 'dp', axis=1, tiled=True)  41.9 us
    all_to_all x1, waiting for transfers between devices, body(): lax.all_to_all(jnp.stack(jnp.split(wanted, lax.axis_size('dp'), axis=2)),...  40.7 us
    dot_general x8, matrix products, single(): jnp.einsum('ra,rb->ab', left_rows, partner_block, preferred_element_type=...  38.6 us
    pmax x1, waiting for transfers between devices, body(): left_all = lax.pmax(left_part, 'dp')  38.6 us
    gather x8, local copies, waits for them, and re-layouts, single(): left_rows = jnp.take(own_full, expert_pick, axis=0)  19.6 us
    all_to_all x1, starting transfers between devices, body(): lax.all_to_all(outbound.reshape((num_devices,) + acts.shape[1:]), 'expert...  12.2 us
  transfers between devices with their start and end apart: 5, of which 5 were waited for; matrix products, arithmetic and copies ran while one was open for 1% of the time, Pallas kernels for 0%

profile of v1, /device:TPU:2, one launch (start us, length us, event | category | flops | bytes accessed | tf_op | source)
XLA Modules:
  0.0 552.1 jit_solution(15554598813296755916)
XLA Ops:
  11.0 3.7 convolution_convert_fusion
  14.7 7.1 %copy.34 = bf16[8,8,64,1536]{3,2,1,0:T(8,128)(2,1)} copy(bf16[8,8,64,1536]{3,1,2,0:T(8,128)(2,1)S(1)} %bitcast.121) | data formatting | bytes 25165824
  21.8 12.2 %all-to-all-start = ((bf16[64,64,1536]{2,1,0:T(8,128)(2,1)}), bf16[64,64,1536]{2,1,0:T(8,128)(2,1)}, u32[]{:S(2)}, u32[]{:S(2)}) async-start(bf16[64,64,1536]{2,1,0:T(8,128)(2,1)} %bitcast.120), calls=%async_computation | async-start | bytes 25165824 | tf_op jit(solution)/shard_map/all_to_all | solution.py:39
  34.1 274.5 %all-to-all-done = bf16[64,64,1536]{2,1,0:T(8,128)(2,1)} async-done(((bf16[64,64,1536]{2,1,0:T(8,128)(2,1)}), bf16[64,64,1536]{2,1,0:T(8,128)(2,1)}, u32[]{:S(2)}, u32[]{:S(2)}) %all-to-all-start) | async-done | bytes 12582944 | tf_op jit(solution)/shard_map/all_to_all | solution.py:39
  308.6 8.1 %gather_fusion.2 = bf16[32,64,1536]{2,1,0:T(8,128)(2,1)} fusion(bf16[64,64,1536]{2,1,0:T(8,128)(2,1)} %all-to-all-done, s32[1024]{0:T(1024)S(1)} %pad_clamp_fusion.2), kind=kCustom, calls=%fused_computation.2 | custom fusion | bytes 12583040 | tf_op jit(solution)/shard_map/jit(_take)/gather | solution.py:46
  316.7 3.4 broadcast_select_fusion
  321.4 3.5 pad_maximum_fusion
  324.9 5.2 all-to-all-start.1
  331.1 41.9 %all-gather.2.cloned.1.call-done = bf16[2,256,1536]{2,1,0:T(8,128)(2,1)} async-done(((bf16[2,64,1536]{2,1,0:T(8,128)(2,1)}), bf16[2,256,1536]{2,1,0:T(8,128)(2,1)}) %all-gather.2.cloned.1.call-update) | async-done | bytes 1572880 | tf_op jit(solution)/shard_map/all_gather | solution.py:36
  374.7 40.7 %all-to-all-done.1 = bf16[4,32,64,384]{3,2,1,0:T(8,128)(2,1)} async-done(((bf16[4,32,64,384]{3,2,1,0:T(8,128)(2,1)}), bf16[4,32,64,384]{3,2,1,0:T(8,128)(2,1)}, u32[]{:S(2)}, u32[]{:S(2)}) %all-to-all-start.1) | async-done | bytes 6291488 | tf_op jit(solution)/shard_map/all_to_all | solution.py:48
  415.4 3.6 copy.17
  419.0 2.7 copy-done.1
  423.7 64.2 %while.12 = (s32[]{:T(128)}, f32[8,4,1536]{2,1,0:T(4,128)S(1)}, f32[8,4,384]{2,1,0:T(4,128)S(1)}, s32[8,4]{1,0:T(8,128)S(1)}, bf16[2,256,1536]{2,1,0:T(8,128)(2,...) while((s32[]{:T(128)}, f32[8,4,1536]{2,1,0:T(4,128)S(1)}, ...), condition=%wide.region_5.6_spmd, body=%wide.region_2.5_spmd.sunk | while | flops 1218975232 | bytes 10461917 | solution.py:84
  426.8 4.8 fusion.37
  434.8 4.8 fusion.37
  442.9 4.8 fusion.37
  450.9 4.8 fusion.37
  458.9 4.8 fusion.37
  466.9 4.8 fusion.37
  475.0 4.8 fusion.37
  483.0 4.8 fusion.37
  488.9 5.8 %all-to-all-start.2 = ((f32[64,1,384]{2,1,0:T(1,128)}), f32[64,1,384]{2,1,0:T(1,128)S(1)}, u32[]{:S(2)}, u32[]{:S(2)}) async-start(f32[64,1,384]{2,1,0:T(1,128)} %copy.18), calls=%async_computation.2 | async-start | bytes 196608 | tf_op jit(solution)/shard_map/all_to_all | solution.py:93
  495.5 8.4 %all-to-all-done.2 = f32[64,1,384]{2,1,0:T(1,128)S(1)} async-done(((f32[64,1,384]{2,1,0:T(1,128)}), f32[64,1,384]{2,1,0:T(1,128)S(1)}, u32[]{:S(2)}, u32[]{:S(2)}) %all-to-all-start.2) | async-done | bytes 98336 | tf_op jit(solution)/shard_map/all_to_all | solution.py:93
  505.2 38.6 %all-reduce.2.cloned.1.call-done = f32[32,1536]{1,0:T(8,128)} async-done(((f32[32,1536]{1,0:T(8,128)}), f32[32,1536]{1,0:T(8,128)}) %all-reduce.2.cloned.1.call-update) | async-done | bytes 196624 | tf_op jit(solution)/shard_map/pmax | solution.py:87
  (115 shorter events, 39.5 us)
Async XLA Ops:
  10.3 4.4 copy-start.2
  21.8 286.8 %all-to-all-start = ((bf16[64,64,1536]{2,1,0:T(8,128)(2,1)}), bf16[64,64,1536]{2,1,0:T(8,128)(2,1)}, u32[]{:S(2)}, u32[]{:S(2)}) async-start(bf16[64,64,1536]{2,1,0:T(8,128)(2,1)} %bitcast.120), calls=%async_computation | async-start | bytes 25165824 | tf_op jit(solution)/shard_map/all_to_all | solution.py:39
  324.9 90.5 %all-to-all-start.1 = ((bf16[4,32,64,384]{3,2,1,0:T(8,128)(2,1)}), bf16[4,32,64,384]{3,2,1,0:T(8,128)(2,1)}, u32[]{:S(2)}, u32[]{:S(2)}) async-start(bf16[4,32,64,384]{3,2,1,0:T(8,128)(2,1)} %pad_maximum_fusion), calls=%async_computation.1 | async-start | bytes 12582912 | tf_op jit(solution)/shard_map/all_to_all | solution.py:48
  330.2 42.8 %all-gather.2.cloned.1.call-start = ((), (), s32[]{:S(2)}) async-start(), calls=%async_computation.3 | async-start | bytes 1966080 | tf_op jit(solution)/shard_map/all_gather | solution.py:36
  419.0 2.7 copy-start.1
  421.7 2.0 copy-start
  488.9 15.0 %all-to-all-start.2 = ((f32[64,1,384]{2,1,0:T(1,128)}), f32[64,1,384]{2,1,0:T(1,128)S(1)}, u32[]{:S(2)}, u32[]{:S(2)}) async-start(f32[64,1,384]{2,1,0:T(1,128)} %copy.18), calls=%async_computation.2 | async-start | bytes 196608 | tf_op jit(solution)/shard_map/all_to_all | solution.py:93
  494.7 49.1 %all-reduce.2.cloned.1.call-start = ((), (), s32[]{:S(2)}) async-start(), calls=%async_computation.4 | async-start | bytes 393216 | tf_op jit(solution)/shard_map/pmax | solution.py:87
Sparse Core Ops, SparseCore 0:
  332.8 40.1 all-gather.1
  497.9 45.8 all-reduce.1
